TPU v7x, 32 devices: a whole 2x2x4 slice. The times are simulated.
32 devices in a mesh: grp: 2 (over x), probe: 8 (over z, y), beam: 2 (over core).
Axes of the slice: x: 2, y: 2, z: 4, core: 2. Of those that a mesh axis runs over, the one named last changes fastest.
Arguments:
- smatrix: bfloat16 [8192, 8, 512], P(('grp', 'beam'), 'probe'), parts along dimension 0, may hold values from -0.09375 to 0.09375
- aperture: float32 [4096], P('beam'), may hold values from 0.5 to 1.5
- aberration: float32 [4096], P('beam'), may hold values from -3.140625 to 3.140625
- beam_k: int32 [2, 4096], P(None, 'beam'), may hold values from -32 to 31, as said below
- probe_pos: int32 [2, 2048], P(None, 'probe'), may hold values from 0 to 1023
- patches: bfloat16 [128, 512], P(('grp', 'probe')), parts along dimension 0, may hold values from -6 to 6
- patch_col: int32 [128], P('grp'), parts along dimension 0, may hold values from 0 to 7, never falling along the last dimension, each value on 1 to 32 neighbouring positions
Outputs:
- ionization: float32 [16, 2048], P('grp', ('probe', 'beam')), parts along dimension 0
There are 2 independent parts, one for each index of `grp`. A program takes and returns all parts, laid end to end along the dimension named above; an argument that names none is the same for every part. Nothing has to cross between parts.
Inputs may be any that keep to these rules, and one draw needn't show every extreme that they name: `patch_col`: patches are ordered by atom column; each of the 8 columns has 1 to 32 patches, and some column has exactly 32. `beam_k`: no two beams have the same pair of indices.
All inputs are finite; a program needn't handle non-finite values.
Results may differ from a plain program's by a relative error of at most 0.005.
Values may be sent and summed in bfloat16 or wider, within the bound.
A program may use at most 128 MiB of HBM per device.

v0:
```python
import math
import jax
import jax.numpy as jnp
from jax import lax
from jax.sharding import PartitionSpec as P

PSIDE = 16
GRID = 1024


def coefficients(beam_k, beam_cos, beam_sin, positions):
    turn_count = (
        positions[0][:, None] * beam_k[0][None, :] + positions[1][:, None] * beam_k[1][None, :]
        & GRID - 1
    )
    quarter = GRID // 4
    quadrant = lax.shift_right_arithmetic(turn_count + quarter // 2, quarter.bit_length() - 1)
    resid = (turn_count - quadrant * quarter).astype(jnp.float32) * (2.0 * math.pi / GRID)
    sq = resid * resid
    sin_r = resid + resid * sq * (
        -1.0 / 6 + sq * (1.0 / 120 + sq * (-1.0 / 5040 + sq * (1.0 / 362880)))
    )
    cos_r = 1.0 + sq * (-0.5 + sq * (1.0 / 24 + sq * (-1.0 / 720 + sq * (1.0 / 40320))))
    odd = quadrant & 1 == 1
    cos_mag = jnp.where(odd, sin_r, cos_r)
    sin_mag = jnp.where(odd, cos_r, sin_r)
    cos_t = jnp.where(quadrant + 1 & 2 != 0, -cos_mag, cos_mag)
    sin_t = jnp.where(quadrant & 2 != 0, -sin_mag, sin_mag)
    real_coef = (beam_cos[None, :] * cos_t - beam_sin[None, :] * sin_t).astype(jnp.bfloat16)
    imag_coef = (-(beam_sin[None, :] * cos_t + beam_cos[None, :] * sin_t)).astype(jnp.bfloat16)
    return (real_coef, imag_coef)


def detector(edge_count):
    half_side = edge_count // 2
    pixel_index = jnp.arange(edge_count * edge_count, dtype=jnp.int32)
    mode_index = jnp.arange(edge_count * half_side, dtype=jnp.int32)
    row_off = pixel_index // edge_count
    col_off = pixel_index % edge_count
    freq_first = mode_index // half_side - half_side
    freq_second = mode_index % half_side - edge_count // 4
    turn_count = jnp.mod(
        row_off[:, None] * freq_first[None, :] + col_off[:, None] * freq_second[None, :], edge_count
    )
    angle_value = 2.0 * math.pi / edge_count * turn_count.astype(jnp.float32)
    real_part = jnp.cos(angle_value)
    imag_part = -jnp.sin(angle_value)
    upper_rows = jnp.concatenate([real_part, imag_part], axis=1)
    lower_rows = jnp.concatenate([-imag_part, real_part], axis=1)
    return jnp.concatenate([upper_rows, lower_rows], axis=0).astype(jnp.bfloat16)


def patch_energy(picked, pot_rows, det_table):
    half_width = pot_rows.shape[-1] // 2
    psi_re = picked[..., :half_width].astype(jnp.float32)
    psi_im = picked[..., half_width:].astype(jnp.float32)
    pot_re = pot_rows[:, :half_width].astype(jnp.float32)
    pot_im = pot_rows[:, half_width:].astype(jnp.float32)
    wave_out = jnp.concatenate(
        [psi_re * pot_re - psi_im * pot_im, psi_re * pot_im + psi_im * pot_re], axis=-1
    ).astype(jnp.bfloat16)
    projected = jnp.einsum("rjx,xq->rjq", wave_out, det_table, preferred_element_type=jnp.float32)
    return jnp.sum(projected * projected, axis=-1) / float(half_width * (det_table.shape[1] // 2))


def combine(beam_terms):
    half_width = beam_terms.shape[-1] // 2
    return jnp.concatenate(
        [
            beam_terms[0, ..., :half_width] - beam_terms[1, ..., half_width:],
            beam_terms[0, ..., half_width:] + beam_terms[1, ..., :half_width],
        ],
        axis=-1,
    )


def spread_patches(psi, all_patches, patch_col, det_table):
    patch_total = all_patches.shape[0]
    group_size = math.gcd(patch_total, 16)
    column_count = psi.shape[1]
    col_groups = patch_col.reshape(patch_total // group_size, group_size)
    pot_groups = all_patches.reshape(patch_total // group_size, group_size, all_patches.shape[1])
    col_range = jnp.arange(column_count, dtype=jnp.int32)

    def add_block(running, blk_pair):
        col_ids, pot_rows = blk_pair
        picked = jnp.take(psi, col_ids, axis=1)
        energy = patch_energy(picked, pot_rows, det_table)
        onehot = (col_ids[:, None] == col_range[None, :]).astype(jnp.float32)
        return (
            running + jnp.einsum("rj,jc->cr", energy, onehot, precision=lax.Precision.HIGHEST),
            None,
        )

    running, _ = lax.scan(
        add_block, jnp.zeros((column_count, psi.shape[0]), jnp.float32), (col_groups, pot_groups)
    )
    return running


def apply_patches(psi_own, all_patches, patch_col, det_table):
    traded = lax.all_to_all(psi_own, "probe", split_axis=0, concat_axis=2, tiled=True)
    return spread_patches(traded[0], all_patches, patch_col, det_table)


def shards(smatrix, aperture, aberration, beam_k, probe_pos, patches, patch_col):
    probe_count = lax.axis_size("probe")
    beam_count = lax.axis_size("beam")
    all_patches = lax.all_gather(patches, "probe", axis=0, tiled=True)
    det_table = detector(PSIDE)
    col_dev = smatrix.shape[1]
    width_two = smatrix.shape[2]
    full_matrix = lax.all_gather(smatrix, "beam", axis=0, tiled=True)
    full_cos = lax.all_gather(aperture * jnp.cos(aberration), "beam", axis=0, tiled=True)
    full_sin = lax.all_gather(aperture * jnp.sin(aberration), "beam", axis=0, tiled=True)
    full_k = lax.all_gather(beam_k, "beam", axis=1, tiled=True)
    all_pos = lax.all_gather(probe_pos, "probe", axis=1, tiled=True)
    all_pos, all_patches = lax.optimization_barrier((all_pos, all_patches))
    probe_total = all_pos.shape[1]
    half_probes = probe_total // (beam_count * probe_count)
    split_pos = all_pos.reshape(2, probe_count, beam_count, half_probes)
    mine = lax.dynamic_slice_in_dim(split_pos, lax.axis_index("beam"), 1, 2).reshape(
        2, probe_count * half_probes
    )
    real_coef, imag_coef = coefficients(full_k, full_cos, full_sin, mine)
    beam_terms = jnp.einsum(
        "kpb,bcx->kpcx",
        jnp.stack([real_coef, imag_coef]),
        full_matrix,
        preferred_element_type=jnp.float32,
    )
    psi_own = (
        combine(beam_terms)
        .astype(jnp.bfloat16)
        .reshape(probe_count, half_probes, col_dev, width_two)
    )
    return apply_patches(psi_own, all_patches, patch_col, det_table)


def solution(mesh):
    placed = (
        P(("grp", "beam"), "probe", None),
        P("beam"),
        P("beam"),
        P(None, "beam"),
        P(None, "probe"),
        P(("grp", "probe"), None),
        P("grp"),
    )
    return jax.shard_map(
        shards, mesh=mesh, in_specs=placed, out_specs=P("grp", ("probe", "beam")), check_vma=False
    )
```

profile of v0, /device:TPU:0, one launch (start us, length us, event | category | flops | bytes accessed | tf_op | source)
XLA Modules:
  0.0 168.4 jit_solution(5774982528233616721)
XLA Ops:
  6.5 0.0 all-gather.2.cloned.1.call-start
  6.5 0.7 all-gather.2.cloned.1.call-update
  7.3 32.6 %all_gather.20 = bf16[64,512]{1,0:T(8,128)(2,1)S(1)} all-gather(bf16[8,512]{1,0:T(8,128)(2,1)} %param.14), channel_id=1, replica_groups=mesh['grp'=2,'probe'=8,'beam'=2] {'probe'}, dimensions={0}, use_global_device_ids=true | all-gather | bytes 73728 | tf_op jit(solution)/shard_map/all_gather | solution.py:109
  39.8 26.2 %all_gather.19 = s32[2,2048]{1,0:T(2,128)S(1)} all-gather(s32[2,256]{1,0:T(2,128)} %param.13), channel_id=1, replica_groups=mesh['grp'=2,'probe'=8,'beam'=2] {'probe'}, dimensions={1}, use_global_device_ids=true | all-gather | bytes 18432 | tf_op jit(solution)/shard_map/all_gather | solution.py:117
  66.1 2.0 %all_gather.21 = s32[2,4096]{1,0:T(2,128)S(1)} all-gather(s32[2,2048]{1,0:T(2,128)} %param.12), channel_id=1, replica_groups=mesh['grp'=2,'probe'=8,'beam'=2] {'beam'}, dimensions={1}, use_global_device_ids=true | all-gather | bytes 49152 | tf_op jit(solution)/shard_map/all_gather | solution.py:116
  68.2 0.8 cosine_multiply_fusion
  68.9 1.8 %all_gather.18 = f32[4096]{0:T(1024)S(1)} all-gather(f32[2048]{0:T(1024)S(1)} %get-tuple-element.96), channel_id=1, replica_groups=mesh['grp'=2,'probe'=8,'beam'=2] {'beam'}, dimensions={0}, use_global_device_ids=true | all-gather | bytes 24576 | tf_op jit(solution)/shard_map/all_gather | solution.py:114
  70.8 1.8 %all_gather.22 = f32[4096]{0:T(1024)S(1)} all-gather(f32[2048]{0:T(1024)S(1)} %get-tuple-element.97), channel_id=1, replica_groups=mesh['grp'=2,'probe'=8,'beam'=2] {'beam'}, dimensions={0}, use_global_device_ids=true | all-gather | bytes 24576 | tf_op jit(solution)/shard_map/all_gather | solution.py:115
  72.6 28.6 %subtract_convert_fusion = (bf16[1,1024,4096]{2,1,0:T(8,128)(2,1)}, bf16[1,1024,4096]{2,1,0:T(8,128)(2,1)}) fusion(f32[4096]{0:T(1024)S(1)} %all_gather.22, f32[4096]{0:T(1024)S(1)} %all_gather.18, s32[4096]{0:T(1024)S(1)} %bitcast.53, s32[1024]{0:T(1024)S(1)} %bitcast.55, s32[4096]{0:T(1024)S(1)} %bitcast.52, s32[1024]{0:T(1024)S(1)} %bitcast.54), kind=kLoop, calls=%fused_computation.60 | loop fusion | flops 209715200 | bytes 16850944 | tf_op jit(solution)/shard_map/convert_element_type | solution.py:29
  101.2 0.0 all-gather.2.cloned.1.call-done
  101.2 13.2 %fusion.37 = f32[2,1024,1,512]{3,1,0,2:T(8,128)S(1)} fusion(bf16[4096,1,512]{2,0,1:T(8,128)(2,1)} %all-gather.2.cloned.1.call-done, bf16[1,1024,4096]{2,1,0:T(8,128)(2,1)} %get-tuple-element.91, bf16[1,1024,4096]{2,1,0:T(8,128)(2,1)} %get-tuple-element.90), kind=kOutput, calls=%fused_computation.68 | convolution fusion | flops 8598323200 | bytes 25165824 | tf_op jit(solution)/shard_map/kpb,bcx->kpcx/dot_general | solution.py:126
  114.4 0.0 copy-start.1
  114.4 0.3 fusion.43
  114.7 1.1 pad_maximum_fusion
  115.7 3.9 %all-to-all-start = ((bf16[8,128,1,512]{3,1,2,0:T(8,128)(2,1)}), bf16[8,128,1,512]{3,1,2,0:T(8,128)(2,1)S(1)}, u32[]{:S(2)}, u32[]{:S(2)}) async-start(bf16[8,128,1,512]{3,1,2,0:T(8,128)(2,1)} %pad_maximum_fusion), calls=%async_computation | async-start | bytes 2097152 | tf_op jit(solution)/shard_map/all_to_all | solution.py:102
  119.6 0.0 copy-done.1
  119.6 0.1 reshape.617
  119.7 0.7 negate_convert_fusion.1
  120.4 25.3 %all-to-all-done = bf16[8,128,1,512]{3,1,2,0:T(8,128)(2,1)S(1)} async-done(((bf16[8,128,1,512]{3,1,2,0:T(8,128)(2,1)}), bf16[8,128,1,512]{3,1,2,0:T(8,128)(2,1)S(1)}, u32[]{:S(2)}, u32[]{:S(2)}) %all-to-all-start) | async-done | bytes 1048608 | tf_op jit(solution)/shard_map/all_to_all | solution.py:102
  145.7 15.3 %while.11 = (s32[]{:T(128)}, f32[8,128]{1,0:T(8,128)S(1)}, s32[4,16]{1,0:T(4,128)S(1)}, bf16[128,8,512]{2,0,1:T(8,128)(2,1)S(1)}, bf16[4,16,512]{2,1,0:T(8,128)(...) while((s32[]{:T(128)}, f32[8,128]{1,0:T(8,128)S(1)}, s32[4,16]{1,0:T(4,128)S(1)}, ...), condition=%wide.region_2.3_spmd.clone, body=%wide.region_0.2_spmd.clone.sunk | while | flops 548613504 | bytes 15086155 | solution.py:95
  145.7 0.7 gather_fusion
  146.4 1.3 fusion.68
  147.7 0.7 fusion.69
  148.4 0.8 multiply_reduce_fusion.2
  149.2 0.2 convolution_add_fusion.2
  149.5 0.7 gather_fusion
  150.2 1.3 fusion.68
  151.6 0.7 fusion.69
  152.3 0.8 multiply_reduce_fusion.2
  153.1 0.2 convolution_add_fusion.2
  153.4 0.7 gather_fusion
  154.1 1.3 fusion.68
  155.4 0.7 fusion.69
  156.1 0.8 multiply_reduce_fusion.2
  156.9 0.2 convolution_add_fusion.2
  157.2 0.7 gather_fusion
  157.9 1.3 fusion.68
  159.2 0.7 fusion.69
  159.9 0.8 multiply_reduce_fusion.2
  160.7 0.2 convolution_add_fusion.2
  160.9 0.0 copy-start
  161.0 0.7 copy-done
  (27 shorter events, 0.4 us)
Async XLA Ops:
  6.5 94.7 %all-gather.2.cloned.1.call-start = ((), (), s32[]{:S(2)}) async-start(), calls=%async_computation.1 | async-start | bytes 6291456 | tf_op jit(solution)/shard_map/all_gather | solution.py:113
  114.4 5.2 %copy-start.1 = (s32[64]{0:T(128)S(1)}, s32[64]{0:T(128)}, u32[]{:S(2)}) copy-start(s32[64]{0:T(128)} %param.15) | copy-start | bytes 772
  115.7 30.0 %all-to-all-start = ((bf16[8,128,1,512]{3,1,2,0:T(8,128)(2,1)}), bf16[8,128,1,512]{3,1,2,0:T(8,128)(2,1)S(1)}, u32[]{:S(2)}, u32[]{:S(2)}) async-start(bf16[8,128,1,512]{3,1,2,0:T(8,128)(2,1)} %pad_maximum_fusion), calls=%async_computation | async-start | bytes 2097152 | tf_op jit(solution)/shard_map/all_to_all | solution.py:102
  160.9 0.7 copy-start
Sparse Core Ops, SparseCore 0:
  8.9 16.3 all-gather.1
where the time goes:
time: 169 us; the launch traced here: 168 us
  blocking collectives  64.5 us (38%)
  other arithmetic  39.6 us (23%)
  waiting for transfers between devices  26 us (15%)
  matrix products  17.2 us (10%)
  between operations  13.5 us (8%)
  starting transfers between devices  3.86 us (2%)
  local copies, waits for them, and re-layouts  3.57 us (2%)
    all_gather x1, blocking collectives, shards(): all_patches = lax.all_gather(patches, 'probe', axis=0, tiled=True)  32.6 us
    convert_element_type x1, other arithmetic, coefficients(): (beam_cos[None, :] * cos_t - beam_sin[None, :] * sin_t).astype(jnp.bfloat16)  28.6 us
    all_gather x1, blocking collectives, shards(): all_pos = lax.all_gather(probe_pos, 'probe', axis=1, tiled=True)  26.2 us
    all_to_all x1, waiting for transfers between devices, apply_patches(): lax.all_to_all(psi_own, 'probe', split_axis=0, concat_axis=2, tiled=True)  25.3 us
    dot_general x1, matrix products, shards(): jnp.einsum('kpb,bcx->kpcx', jnp.stack([real_coef, imag_coef]), full_matri...  13.2 us
    select_n x8, other arithmetic, add_block(): picked = jnp.take(psi, col_ids, axis=1)  5.24 us
    all_to_all x1, starting transfers between devices, apply_patches(): lax.all_to_all(psi_own, 'probe', split_axis=0, concat_axis=2, tiled=True)  3.86 us
    another operation x6, other arithmetic  3.72 us
  transfers between devices with their start and end apart: 2, of which 1 were waited for; matrix products, arithmetic and copies ran while one was open for 18% of the time, Pallas kernels for 0%

commit v1 on v0

--- a/solution.py
+++ b/solution.py
@@ -6,6 +6,19 @@
 
 PSIDE = 16
 GRID = 1024
+
+
+def ring_gather(shard, axis, dim):
+    ways = lax.axis_size(axis)
+    up = [(d, (d + 1) % ways) for d in range(ways)]
+    down = [(d, (d - 1) % ways) for d in range(ways)]
+    earlier, later = ([shard], [shard])
+    for _ in range(ways // 2):
+        earlier.append(lax.ppermute(earlier[-1], axis, up))
+    for _ in range((ways - 1) // 2):
+        later.append(lax.ppermute(later[-1], axis, down))
+    line = jnp.concatenate([*earlier[::-1], *later[1:]], axis=dim)
+    return jnp.roll(line, (lax.axis_index(axis) - ways // 2) * shard.shape[dim], axis=dim)
 
 
 def coefficients(beam_k, beam_cos, beam_sin, positions):
@@ -106,7 +119,7 @@
 def shards(smatrix, aperture, aberration, beam_k, probe_pos, patches, patch_col):
     probe_count = lax.axis_size("probe")
     beam_count = lax.axis_size("beam")
-    all_patches = lax.all_gather(patches, "probe", axis=0, tiled=True)
+    all_patches = ring_gather(patches, "probe", 0)
     det_table = detector(PSIDE)
     col_dev = smatrix.shape[1]
     width_two = smatrix.shape[2]

time: 169 us -> 154 us (0.911)
  blocking collectives: 64.5 us -> 32 us
  starting transfers between devices: 3.86 us -> 20.1 us
    all_gather x1 -> x0, blocking collectives: 32.6 us -> none  [shards(): all_patches = lax.all_gather(patches, 'probe', axis=0, tiled=True)]
    ppermute x0 -> x7, starting transfers between devices: none -> 13.9 us  [the longest x3 10.8 us: ring_gather(): later.append(lax.ppermute(later[-1], axis, down))]
    ppermute x0 -> x7, waiting for transfers between devices: none -> 6.2 us  [the longest x4 5.55 us: ring_gather(): earlier.append(lax.ppermute(earlier[-1], axis, up))]
    all_to_all x1, waiting for transfers between devices: 25.3 us -> 19.8 us  [apply_patches(): lax.all_to_all(psi_own, 'probe', split_axis=0, concat_axis=2, tiled=True)]
    all_to_all x1, starting transfers between devices: 3.86 us -> 6.26 us  [apply_patches(): lax.all_to_all(psi_own, 'probe', split_axis=0, concat_axis=2, tiled=True)]
  transfers between devices with their start and end apart: 2 -> 9, of which waited for: 1 -> 3; matrix products, arithmetic and copies ran while one was open for 18% -> 21% of each run, Pallas kernels for 0% -> 0%
where the time goes in v1:
time: 154 us
  other arithmetic  39.6 us (26%)
  blocking collectives  32 us (21%)
  waiting for transfers between devices  26.1 us (17%)
  starting transfers between devices  20.1 us (13%)
  matrix products  17.2 us (11%)
  between operations  13.5 us (9%)
  local copies, waits for them, and re-layouts  5.01 us (3%)
    convert_element_type x1, other arithmetic, coefficients(): (beam_cos[None, :] * cos_t - beam_sin[None, :] * sin_t).astype(jnp.bfloat16)  28.6 us
    all_gather x1, blocking collectives, shards(): all_pos = lax.all_gather(probe_pos, 'probe', axis=1, tiled=True)  26.3 us
    all_to_all x1, waiting for transfers between devices, apply_patches(): lax.all_to_all(psi_own, 'probe', split_axis=0, concat_axis=2, tiled=True)  19.8 us
    dot_general x1, matrix products, shards(): jnp.einsum('kpb,bcx->kpcx', jnp.stack([real_coef, imag_coef]), full_matri...  13.2 us
    ppermute x3, starting transfers between devices, ring_gather(): later.append(lax.ppermute(later[-1], axis, down))  10.8 us
    all_to_all x1, starting transfers between devices, apply_patches(): lax.all_to_all(psi_own, 'probe', split_axis=0, concat_axis=2, tiled=True)  6.26 us
    ppermute x4, waiting for transfers between devices, ring_gather(): earlier.append(lax.ppermute(earlier[-1], axis, up))  5.55 us
    select_n x8, other arithmetic, add_block(): picked = jnp.take(psi, col_ids, axis=1)  5.24 us
  transfers between devices with their start and end apart: 9, of which 3 were waited for; matrix products, arithmetic and copies ran while one was open for 21% of the time, Pallas kernels for 0%

profile of v1, /device:TPU:0, one launch (start us, length us, event | category | flops | bytes accessed | tf_op | source)
XLA Modules:
  0.0 153.8 jit_solution(12578288067323097044)
XLA Ops:
  6.5 0.0 all-gather.2.cloned.1.call-start
  6.5 3.0 %collective-permute-start = (bf16[8,512]{1,0:T(8,128)(2,1)}, bf16[8,512]{1,0:T(8,128)(2,1)S(1)}, u32[]{:S(2)}, u32[]{:S(2)}) collective-permute-start(bf16[8,512]{1,0:T(8,128)(2,1)} %param.14), channel_id=1, source_target_pairs={{0,2},{2,4},{4,6},{6,8},{8,10},{10,12},{12,14},{14,0},{1,3},{3,5},... | collective-permute-start | bytes 24584 | tf_op jit(solution)/shard_map/ppermute | solution.py:17
  9.5 3.0 %collective-permute-start.4 = (bf16[8,512]{1,0:T(8,128)(2,1)}, bf16[8,512]{1,0:T(8,128)(2,1)S(1)}, u32[]{:S(2)}, u32[]{:S(2)}) collective-permute-start(bf16[8,512]{1,0:T(8,128)(2,1)} %param.14), channel_id=1, source_target_pairs={{0,14},{2,0},{4,2},{6,4},{8,6},{10,8},{12,10},{14,12},{1,15},{3,1}... | collective-permute-start | bytes 24584 | tf_op jit(solution)/shard_map/ppermute | solution.py:19
  12.6 0.0 all-gather.2.cloned.1.call-update
  12.6 2.0 %all_gather.17 = s32[2,4096]{1,0:T(2,128)S(1)} all-gather(s32[2,2048]{1,0:T(2,128)} %param.12), channel_id=1, replica_groups=mesh['grp'=2,'probe'=8,'beam'=2] {'beam'}, dimensions={1}, use_global_device_ids=true | all-gather | bytes 49152 | tf_op jit(solution)/shard_map/all_gather | solution.py:129
  14.7 0.0 collective-permute-done
  14.7 0.1 collective-permute-start.1
  14.7 0.8 cosine_multiply_fusion
  15.5 5.5 %collective-permute-done.1 = bf16[8,512]{1,0:T(8,128)(2,1)S(1)} collective-permute-done((bf16[8,512]{1,0:T(8,128)(2,1)S(1)}, bf16[8,512]{1,0:T(8,128)(2,1)S(1)}, u32[]{:S(2)}, u32[]{:S(2)}) %collective-permute-start.1) | collective-permute-done | bytes 8224 | tf_op jit(solution)/shard_map/ppermute | solution.py:17
  21.1 0.0 collective-permute-start.2
  21.1 1.8 %all_gather.15 = f32[4096]{0:T(1024)S(1)} all-gather(f32[2048]{0:T(1024)S(1)} %get-tuple-element.96), channel_id=1, replica_groups=mesh['grp'=2,'probe'=8,'beam'=2] {'beam'}, dimensions={0}, use_global_device_ids=true | all-gather | bytes 24576 | tf_op jit(solution)/shard_map/all_gather | solution.py:127
  22.9 1.8 %all_gather.18 = f32[4096]{0:T(1024)S(1)} all-gather(f32[2048]{0:T(1024)S(1)} %get-tuple-element.97), channel_id=1, replica_groups=mesh['grp'=2,'probe'=8,'beam'=2] {'beam'}, dimensions={0}, use_global_device_ids=true | all-gather | bytes 24576 | tf_op jit(solution)/shard_map/all_gather | solution.py:128
  24.7 0.0 collective-permute-done.4
  24.7 4.8 %collective-permute-start.5 = (bf16[8,512]{1,0:T(8,128)(2,1)S(1)}, bf16[8,512]{1,0:T(8,128)(2,1)S(1)}, u32[]{:S(2)}, u32[]{:S(2)}) collective-permute-start(bf16[8,512]{1,0:T(8,128)(2,1)S(1)} %collective-permute-done.4), channel_id=1, source_target_pairs={{0,14},{2,0},{4,2},{6,4},{8,6},{10,8},{12,10},{14,12},{1,15},{3,1}... | collective-permute-start | bytes 24584 | tf_op jit(solution)/shard_map/ppermute | solution.py:19
  29.5 0.0 collective-permute-done.2
  29.5 0.0 collective-permute-start.3
  29.5 26.3 %all_gather.16 = s32[2,2048]{1,0:T(2,128)S(1)} all-gather(s32[2,256]{1,0:T(2,128)} %param.13), channel_id=1, replica_groups=mesh['grp'=2,'probe'=8,'beam'=2] {'probe'}, dimensions={1}, use_global_device_ids=true | all-gather | bytes 18432 | tf_op jit(solution)/shard_map/all_gather | solution.py:130
  55.8 0.0 collective-permute-done.5
  55.8 3.0 %collective-permute-start.6 = (bf16[8,512]{1,0:T(8,128)(2,1)S(1)}, bf16[8,512]{1,0:T(8,128)(2,1)S(1)}, u32[]{:S(2)}, u32[]{:S(2)}) collective-permute-start(bf16[8,512]{1,0:T(8,128)(2,1)S(1)} %collective-permute-done.5), channel_id=1, source_target_pairs={{0,14},{2,0},{4,2},{6,4},{8,6},{10,8},{12,10},{14,12},{1,15},{3,1}... | collective-permute-start | bytes 24584 | tf_op jit(solution)/shard_map/ppermute | solution.py:19
  58.9 0.0 collective-permute-done.3
  58.9 0.7 constant_dynamic-update-slice_fusion.11
  59.6 0.6 collective-permute-done.6
  60.2 0.7 constant_dynamic-update-slice_fusion.3
  61.0 28.6 %subtract_convert_fusion = (bf16[1,1024,4096]{2,1,0:T(8,128)(2,1)}, bf16[1,1024,4096]{2,1,0:T(8,128)(2,1)}) fusion(f32[4096]{0:T(1024)S(1)} %all_gather.18, f32[4096]{0:T(1024)S(1)} %all_gather.15, s32[4096]{0:T(1024)S(1)} %bitcast.53, s32[1024]{0:T(1024)S(1)} %bitcast.55, s32[4096]{0:T(1024)S(1)} %bitcast.52, s32[1024]{0:T(1024)S(1)} %bitcast.54), kind=kLoop, calls=%fused_computation.60 | loop fusion | flops 209715200 | bytes 16850944 | tf_op jit(solution)/shard_map/convert_element_type | solution.py:42
  89.6 0.0 all-gather.2.cloned.1.call-done
  89.6 13.2 %fusion.37 = f32[2,1024,1,512]{3,1,0,2:T(8,128)S(1)} fusion(bf16[4096,1,512]{2,0,1:T(8,128)(2,1)} %all-gather.2.cloned.1.call-done, bf16[1,1024,4096]{2,1,0:T(8,128)(2,1)} %get-tuple-element.91, bf16[1,1024,4096]{2,1,0:T(8,128)(2,1)} %get-tuple-element.90), kind=kOutput, calls=%fused_computation.68 | convolution fusion | flops 8598323200 | bytes 25165824 | tf_op jit(solution)/shard_map/kpb,bcx->kpcx/dot_general | solution.py:139
  102.8 0.0 copy-start.1
  102.8 0.3 fusion.43
  103.1 1.1 pad_maximum_fusion
  104.1 6.3 %all-to-all-start = ((bf16[8,128,1,512]{3,1,2,0:T(8,128)(2,1)}), bf16[8,128,1,512]{3,1,2,0:T(8,128)(2,1)S(1)}, u32[]{:S(2)}, u32[]{:S(2)}) async-start(bf16[8,128,1,512]{3,1,2,0:T(8,128)(2,1)} %pad_maximum_fusion), calls=%async_computation | async-start | bytes 2097152 | tf_op jit(solution)/shard_map/all_to_all | solution.py:115
  110.4 0.0 copy-done.1
  110.4 0.1 reshape.617
  110.5 0.7 negate_convert_fusion.1
  111.2 19.8 %all-to-all-done = bf16[8,128,1,512]{3,1,2,0:T(8,128)(2,1)S(1)} async-done(((bf16[8,128,1,512]{3,1,2,0:T(8,128)(2,1)}), bf16[8,128,1,512]{3,1,2,0:T(8,128)(2,1)S(1)}, u32[]{:S(2)}, u32[]{:S(2)}) %all-to-all-start) | async-done | bytes 1048608 | tf_op jit(solution)/shard_map/all_to_all | solution.py:115
  131.0 15.3 %while.11 = (s32[]{:T(128)}, f32[8,128]{1,0:T(8,128)S(1)}, s32[4,16]{1,0:T(4,128)S(1)}, bf16[128,8,512]{2,0,1:T(8,128)(2,1)S(1)}, bf16[4,16,512]{2,1,0:T(8,128)(...) while((s32[]{:T(128)}, f32[8,128]{1,0:T(8,128)S(1)}, s32[4,16]{1,0:T(4,128)S(1)}, ...), condition=%wide.region_2.3_spmd.clone, body=%wide.region_0.2_spmd.clone.sunk | while | flops 548613504 | bytes 15086155 | solution.py:108
  131.1 0.7 gather_fusion
  131.8 1.3 fusion.68
  133.1 0.7 fusion.69
  133.8 0.8 multiply_reduce_fusion.2
  134.6 0.2 convolution_add_fusion.2
  134.9 0.7 gather_fusion
  135.6 1.3 fusion.68
  136.9 0.7 fusion.69
  137.6 0.8 multiply_reduce_fusion.2
  138.4 0.2 convolution_add_fusion.2
  138.7 0.7 gather_fusion
  139.4 1.3 fusion.68
  140.8 0.7 fusion.69
  141.5 0.8 multiply_reduce_fusion.2
  142.2 0.2 convolution_add_fusion.2
  142.5 0.7 gather_fusion
  143.3 1.3 fusion.68
  144.6 0.7 fusion.69
  145.3 0.8 multiply_reduce_fusion.2
  146.1 0.2 convolution_add_fusion.2
  146.3 0.0 copy-start
  146.3 0.7 copy-done
  (42 shorter events, 0.4 us)
Async XLA Ops:
  6.5 83.1 %all-gather.2.cloned.1.call-start = ((), (), s32[]{:S(2)}) async-start(), calls=%async_computation.1 | async-start | bytes 6291456 | tf_op jit(solution)/shard_map/all_gather | solution.py:126
  6.5 8.1 %collective-permute-start = (bf16[8,512]{1,0:T(8,128)(2,1)}, bf16[8,512]{1,0:T(8,128)(2,1)S(1)}, u32[]{:S(2)}, u32[]{:S(2)}) collective-permute-start(bf16[8,512]{1,0:T(8,128)(2,1)} %param.14), channel_id=1, source_target_pairs={{0,2},{2,4},{4,6},{6,8},{8,10},{10,12},{12,14},{14,0},{1,3},{3,5},... | collective-permute-start | bytes 24584 | tf_op jit(solution)/shard_map/ppermute | solution.py:17
  9.5 15.2 %collective-permute-start.4 = (bf16[8,512]{1,0:T(8,128)(2,1)}, bf16[8,512]{1,0:T(8,128)(2,1)S(1)}, u32[]{:S(2)}, u32[]{:S(2)}) collective-permute-start(bf16[8,512]{1,0:T(8,128)(2,1)} %param.14), channel_id=1, source_target_pairs={{0,14},{2,0},{4,2},{6,4},{8,6},{10,8},{12,10},{14,12},{1,15},{3,1}... | collective-permute-start | bytes 24584 | tf_op jit(solution)/shard_map/ppermute | solution.py:19
  14.7 6.4 %collective-permute-start.1 = (bf16[8,512]{1,0:T(8,128)(2,1)S(1)}, bf16[8,512]{1,0:T(8,128)(2,1)S(1)}, u32[]{:S(2)}, u32[]{:S(2)}) collective-permute-start(bf16[8,512]{1,0:T(8,128)(2,1)S(1)} %collective-permute-done), channel_id=1, source_target_pairs={{0,2},{2,4},{4,6},{6,8},{8,10},{10,12},{12,14},{14,0},{1,3},{3,5},... | collective-permute-start | bytes 24584 | tf_op jit(solution)/shard_map/ppermute | solution.py:17
  21.1 8.4 %collective-permute-start.2 = (bf16[8,512]{1,0:T(8,128)(2,1)S(1)}, bf16[8,512]{1,0:T(8,128)(2,1)S(1)}, u32[]{:S(2)}, u32[]{:S(2)}) collective-permute-start(bf16[8,512]{1,0:T(8,128)(2,1)S(1)} %collective-permute-done.1), channel_id=1, source_target_pairs={{0,2},{2,4},{4,6},{6,8},{8,10},{10,12},{12,14},{14,0},{1,3},{3,5},... | collective-permute-start | bytes 24584 | tf_op jit(solution)/shard_map/ppermute | solution.py:17
  24.7 31.1 %collective-permute-start.5 = (bf16[8,512]{1,0:T(8,128)(2,1)S(1)}, bf16[8,512]{1,0:T(8,128)(2,1)S(1)}, u32[]{:S(2)}, u32[]{:S(2)}) collective-permute-start(bf16[8,512]{1,0:T(8,128)(2,1)S(1)} %collective-permute-done.4), channel_id=1, source_target_pairs={{0,14},{2,0},{4,2},{6,4},{8,6},{10,8},{12,10},{14,12},{1,15},{3,1}... | collective-permute-start | bytes 24584 | tf_op jit(solution)/shard_map/ppermute | solution.py:19
  29.5 29.3 %collective-permute-start.3 = (bf16[8,512]{1,0:T(8,128)(2,1)S(1)}, bf16[8,512]{1,0:T(8,128)(2,1)S(1)}, u32[]{:S(2)}, u32[]{:S(2)}) collective-permute-start(bf16[8,512]{1,0:T(8,128)(2,1)S(1)} %collective-permute-done.2), channel_id=1, source_target_pairs={{0,2},{2,4},{4,6},{6,8},{8,10},{10,12},{12,14},{14,0},{1,3},{3,5},... | collective-permute-start | bytes 24584 | tf_op jit(solution)/shard_map/ppermute | solution.py:17
  55.8 4.4 %collective-permute-start.6 = (bf16[8,512]{1,0:T(8,128)(2,1)S(1)}, bf16[8,512]{1,0:T(8,128)(2,1)S(1)}, u32[]{:S(2)}, u32[]{:S(2)}) collective-permute-start(bf16[8,512]{1,0:T(8,128)(2,1)S(1)} %collective-permute-done.5), channel_id=1, source_target_pairs={{0,14},{2,0},{4,2},{6,4},{8,6},{10,8},{12,10},{14,12},{1,15},{3,1}... | collective-permute-start | bytes 24584 | tf_op jit(solution)/shard_map/ppermute | solution.py:19
  102.8 7.6 %copy-start.1 = (s32[64]{0:T(128)S(1)}, s32[64]{0:T(128)}, u32[]{:S(2)}) copy-start(s32[64]{0:T(128)} %param.15) | copy-start | bytes 772
  104.1 26.9 %all-to-all-start = ((bf16[8,128,1,512]{3,1,2,0:T(8,128)(2,1)}), bf16[8,128,1,512]{3,1,2,0:T(8,128)(2,1)S(1)}, u32[]{:S(2)}, u32[]{:S(2)}) async-start(bf16[8,128,1,512]{3,1,2,0:T(8,128)(2,1)} %pad_maximum_fusion), calls=%async_computation | async-start | bytes 2097152 | tf_op jit(solution)/shard_map/all_to_all | solution.py:115
  146.3 0.7 copy-start
Sparse Core Ops, SparseCore 0:
  12.7 12.5 all-gather.1
